TPU v7x, 32 devices: a whole 2x2x4 slice. The times are simulated.
32 devices in a mesh: batch: 4 (over y, x), ctx: 4 (over z), wt: 2 (over core).
Axes of the slice: x: 2, y: 2, z: 4, core: 2. Of those that a mesh axis runs over, the one named last changes fastest.
Arguments:
- inputs: bfloat16 [8, 512, 768], P(('batch', 'wt'), 'ctx'), may hold values from -6 to 6
- prefix_keys: bfloat16 [8, 20, 768], P(('batch', 'wt')), may hold values from -8 to 8
- prefix_values: bfloat16 [8, 20, 768], P(('batch', 'wt')), may hold values from -6 to 6
- gain_attn: bfloat16 [768], P('wt'), may hold values from 0.099609375 to 1.8984375
- w_query: bfloat16 [768, 768], P('wt'), may hold values from -0.02734375 to 0.02734375
- w_key: bfloat16 [768, 768], P('wt'), may hold values from -0.21875 to 0.21875
- w_value: bfloat16 [768, 768], P('wt'), may hold values from -0.21875 to 0.21875
- w_out: bfloat16 [768, 768], P('wt'), may hold values from -2.5 to 2.5
- bias_table: bfloat16 [32, 12], P('wt'), may hold values from -5 to 5
- gain_ffn: bfloat16 [768], P('wt'), may hold values from 0.099609375 to 1.8984375
- w_in: bfloat16 [768, 3072], P('wt'), may hold values from -0.21875 to 0.21875
- w_back: bfloat16 [3072, 768], P('wt'), may hold values from -0.15625 to 0.15625
- buckets: int32 [1023], replicated, may hold values from 0 to 31
- out_grad: bfloat16 [8, 512, 768], P(('batch', 'wt'), 'ctx'), may hold values from -6 to 6
Outputs:
- outputs: bfloat16 [8, 512, 768], P(('batch', 'wt'), 'ctx')
- grad_inputs: bfloat16 [8, 512, 768], P(('batch', 'wt'), 'ctx')
- grad_prefix_keys: float32 [8, 20, 768], P(('batch', 'wt'))
- grad_prefix_values: float32 [8, 20, 768], P(('batch', 'wt'))
- grad_gain_attn: float32 [768], P('wt')
- grad_gain_ffn: float32 [768], P('wt')
- grad_bias_table: float32 [32, 12], P('wt')
- grad_query: float32 [768, 768], P('wt')
- grad_key: float32 [768, 768], P('wt')
- grad_value: float32 [768, 768], P('wt')
- grad_out: float32 [768, 768], P('wt')
- grad_in: float32 [768, 3072], P('wt')
- grad_back: float32 [3072, 768], P('wt')
All inputs are finite; a program needn't handle non-finite values.
Results may differ from a plain program's by a relative error of at most 0.028.
Values may be sent and summed in bfloat16 or wider, within the bound.
No kernel may reach another device: no remote copies, remote signals or barrier semaphores. Data moves between devices by JAX's collectives and lax.ppermute only.
A program may use at most 128 MiB of HBM per device.

v0:
```python
import jax
import jax.numpy as jnp
from jax import lax
from jax.sharding import PartitionSpec as P

KB = 256
EPS = 1e-06


def times_t(left, right):
    return lax.dot_general(
        left, right, (((1,), (1,)), ((), ())), preferred_element_type=jnp.float32
    )


def t_times(left, right):
    return lax.dot_general(
        left, right, (((0,), (0,)), ((), ())), preferred_element_type=jnp.float32
    )


def norm_parts(values):
    inverse = lax.rsqrt(jnp.mean(values * values, axis=-1, keepdims=True) + EPS)
    return (values * inverse, inverse)


def norm_back(grad_norm, gain, scaled, inverse):
    grad_scaled = grad_norm * gain
    return inverse * (grad_scaled - scaled * jnp.mean(grad_scaled * scaled, axis=-1, keepdims=True))


def smooth_act(values):
    return jax.nn.gelu(values, approximate=True)


def shards(
    inputs,
    prefix_keys,
    prefix_values,
    gain_attn,
    w_query,
    w_key,
    w_value,
    w_out,
    bias_table,
    gain_ffn,
    w_in,
    w_back,
    buckets,
    out_grad,
):
    wq, wk, wv, wo, gain_one, table = (
        lax.all_gather(w_query, "wt", axis=0, tiled=True),
        lax.all_gather(w_key, "wt", axis=0, tiled=True),
        lax.all_gather(w_value, "wt", axis=0, tiled=True),
        lax.all_gather(w_out, "wt", axis=0, tiled=True),
        lax.all_gather(gain_attn, "wt", axis=0, tiled=True),
        lax.all_gather(bias_table, "wt", axis=0, tiled=True),
    )
    w_first, w_second, gain_two = (
        lax.all_gather(w_in, "wt", axis=0, tiled=True),
        lax.all_gather(w_back, "wt", axis=0, tiled=True),
        lax.all_gather(gain_ffn, "wt", axis=0, tiled=True),
    )
    tokens = inputs[0].astype(jnp.float32)
    rows, width = tokens.shape
    heads = table.shape[1]
    nbuck = table.shape[0]
    hsize = width // heads
    memory = prefix_keys.shape[1]
    keys_mem = prefix_keys[0].reshape(memory, heads, hsize)
    vals_mem = prefix_values[0].reshape(memory, heads, hsize)
    scaled1, inverse1 = norm_parts(tokens)
    normed1 = (scaled1 * gain_one.astype(jnp.float32)).astype(jnp.bfloat16)
    query = jnp.dot(normed1, wq, preferred_element_type=jnp.float32).astype(jnp.bfloat16)
    keys = jnp.dot(normed1, wk, preferred_element_type=jnp.float32).astype(jnp.bfloat16)
    vals = jnp.dot(normed1, wv, preferred_element_type=jnp.float32).astype(jnp.bfloat16)
    key_full, value_full = (
        lax.all_gather(keys, "ctx", axis=0, tiled=True),
        lax.all_gather(vals, "ctx", axis=0, tiled=True),
    )
    length = key_full.shape[0]
    starts = jnp.arange(length // KB, dtype=jnp.int32) * KB
    bucket_range = jnp.arange(nbuck, dtype=jnp.int32)
    positions = lax.axis_index("ctx") * rows + jnp.arange(rows, dtype=jnp.int32)
    qheads = query.reshape(rows, heads, hsize)

    def scores_at(start, key_all):
        key_block = lax.dynamic_slice_in_dim(key_all, start, KB, 0).reshape(KB, heads, hsize)
        cols = start + jnp.arange(KB, dtype=jnp.int32)
        where = cols[None, :] - positions[:, None] + (length - 1)
        bucket_ids = buckets[where]
        bucket_map = (bucket_ids[:, :, None] == bucket_range[None, None, :]).astype(jnp.bfloat16)
        bias = jnp.einsum("qkb,bh->hqk", bucket_map, table, preferred_element_type=jnp.float32)
        raw = jnp.einsum("qhd,khd->hqk", qheads, key_block, preferred_element_type=jnp.float32)
        return (raw + bias, bucket_map, key_block)

    mem_scores = jnp.einsum("qhd,khd->hqk", qheads, keys_mem, preferred_element_type=jnp.float32)
    top_start = jnp.max(mem_scores, axis=2)
    total_start = jnp.sum(jnp.exp(mem_scores - top_start[:, :, None]), axis=2)

    def stat_step(carry, start):
        top, total = carry
        block, _, _ = scores_at(start, key_full)
        new_top = jnp.maximum(top, jnp.max(block, axis=2))
        total = total * jnp.exp(top - new_top) + jnp.sum(
            jnp.exp(block - new_top[:, :, None]), axis=2
        )
        return ((new_top, total), None)

    (top, total), _ = lax.scan(stat_step, (top_start, total_start), starts)
    mem_prob = jnp.exp(mem_scores - top[:, :, None]) / total[:, :, None]
    mem_low = mem_prob.astype(jnp.bfloat16)
    mixed_start = jnp.einsum("hqk,khd->qhd", mem_low, vals_mem, preferred_element_type=jnp.float32)

    def out_step(acc, start):
        block, _, _ = scores_at(start, key_full)
        prob = (jnp.exp(block - top[:, :, None]) / total[:, :, None]).astype(jnp.bfloat16)
        value_block = lax.dynamic_slice_in_dim(value_full, start, KB, 0).reshape(KB, heads, hsize)
        return (
            acc + jnp.einsum("hqk,khd->qhd", prob, value_block, preferred_element_type=jnp.float32),
            None,
        )

    mixed, _ = lax.scan(out_step, mixed_start, starts)
    attended = mixed.reshape(rows, width).astype(jnp.bfloat16)
    hidden = tokens + jnp.dot(attended, wo, preferred_element_type=jnp.float32)
    scaled2, inverse2 = norm_parts(hidden)
    normed2 = (scaled2 * gain_two.astype(jnp.float32)).astype(jnp.bfloat16)
    inner = jnp.dot(normed2, w_first, preferred_element_type=jnp.float32)
    act_value, act_pull = jax.vjp(smooth_act, inner)
    act_out = act_value.astype(jnp.bfloat16)
    result = hidden + jnp.dot(act_out, w_second, preferred_element_type=jnp.float32)
    wq, wk, wv, wo, gain_one = (
        lax.all_gather(w_query, "wt", axis=0, tiled=True),
        lax.all_gather(w_key, "wt", axis=0, tiled=True),
        lax.all_gather(w_value, "wt", axis=0, tiled=True),
        lax.all_gather(w_out, "wt", axis=0, tiled=True),
        lax.all_gather(gain_attn, "wt", axis=0, tiled=True),
    )
    w_first, w_second, gain_two = (
        lax.all_gather(w_in, "wt", axis=0, tiled=True),
        lax.all_gather(w_back, "wt", axis=0, tiled=True),
        lax.all_gather(gain_ffn, "wt", axis=0, tiled=True),
    )
    key_back, value_back = (
        lax.all_gather(keys, "ctx", axis=0, tiled=True),
        lax.all_gather(vals, "ctx", axis=0, tiled=True),
    )
    cotangent = out_grad[0]
    grad_second = t_times(act_out, cotangent)
    grad_act = times_t(cotangent, w_second).astype(jnp.bfloat16)
    grad_inner = act_pull(grad_act.astype(jnp.float32))[0].astype(jnp.bfloat16)
    grad_first = t_times(normed2, grad_inner)
    grad_normed2 = times_t(grad_inner, w_first)
    grad_gain_two = jnp.sum(grad_normed2 * scaled2, axis=0)
    grad_hidden = cotangent.astype(jnp.float32) + norm_back(
        grad_normed2, gain_two.astype(jnp.float32), scaled2, inverse2
    )
    part_first, part_second, part_gain_two = (
        lax.psum_scatter(
            grad_first.astype(jnp.bfloat16), "wt", scatter_dimension=0, tiled=True
        ).astype(jnp.float32),
        lax.psum_scatter(
            grad_second.astype(jnp.bfloat16), "wt", scatter_dimension=0, tiled=True
        ).astype(jnp.float32),
        lax.psum_scatter(
            grad_gain_two.astype(jnp.bfloat16), "wt", scatter_dimension=0, tiled=True
        ).astype(jnp.float32),
    )
    grad_branch = grad_hidden.astype(jnp.bfloat16)
    grad_wo = t_times(attended, grad_branch)
    grad_mixed = times_t(grad_branch, wo).astype(jnp.bfloat16).reshape(rows, heads, hsize)
    spread = jnp.einsum("qhd,qhd->hq", grad_mixed.astype(jnp.float32), mixed)
    mem_dprob = jnp.einsum("qhd,khd->hqk", grad_mixed, vals_mem, preferred_element_type=jnp.float32)
    mem_dscore = (mem_prob * (mem_dprob - spread[:, :, None])).astype(jnp.bfloat16)
    grad_q_start = jnp.einsum(
        "hqk,khd->qhd", mem_dscore, keys_mem, preferred_element_type=jnp.float32
    )
    grad_mem_keys = jnp.einsum(
        "hqk,qhd->khd", mem_dscore, qheads, preferred_element_type=jnp.float32
    ).reshape(memory, width)
    grad_mem_values = jnp.einsum(
        "hqk,qhd->khd", mem_low, grad_mixed, preferred_element_type=jnp.float32
    ).reshape(memory, width)

    def grad_step(carry, start):
        grad_q, table_acc = carry
        block, bucket_map, key_block = scores_at(start, key_back)
        prob = jnp.exp(block - top[:, :, None]) / total[:, :, None]
        value_block = lax.dynamic_slice_in_dim(value_back, start, KB, 0).reshape(KB, heads, hsize)
        grad_prob = jnp.einsum(
            "qhd,khd->hqk", grad_mixed, value_block, preferred_element_type=jnp.float32
        )
        grad_score = (prob * (grad_prob - spread[:, :, None])).astype(jnp.bfloat16)
        grad_q = grad_q + jnp.einsum(
            "hqk,khd->qhd", grad_score, key_block, preferred_element_type=jnp.float32
        )
        grad_kblock = jnp.einsum(
            "hqk,qhd->khd", grad_score, qheads, preferred_element_type=jnp.float32
        ).reshape(KB, width)
        grad_vblock = jnp.einsum(
            "hqk,qhd->khd",
            prob.astype(jnp.bfloat16),
            grad_mixed,
            preferred_element_type=jnp.float32,
        ).reshape(KB, width)
        table_acc = table_acc + jnp.einsum(
            "hqk,qkb->bh", grad_score, bucket_map, preferred_element_type=jnp.float32
        )
        return ((grad_q, table_acc), (grad_kblock, grad_vblock))

    zero_table = jnp.zeros((nbuck, heads), jnp.float32)
    (grad_q, grad_table), (grad_kblocks, grad_vblocks) = lax.scan(
        grad_step, (grad_q_start, zero_table), starts
    )
    grad_key_all = grad_kblocks.reshape(length, width)
    grad_value_all = grad_vblocks.reshape(length, width)
    grad_key_own, grad_value_own = (
        lax.psum_scatter(
            grad_key_all.astype(jnp.bfloat16), "ctx", scatter_dimension=0, tiled=True
        ).astype(jnp.float32),
        lax.psum_scatter(
            grad_value_all.astype(jnp.bfloat16), "ctx", scatter_dimension=0, tiled=True
        ).astype(jnp.float32),
    )
    mem_key_total, mem_value_total = (
        lax.psum(grad_mem_keys.astype(jnp.bfloat16), "ctx").astype(jnp.float32),
        lax.psum(grad_mem_values.astype(jnp.bfloat16), "ctx").astype(jnp.float32),
    )
    grad_q_low = grad_q.reshape(rows, width).astype(jnp.bfloat16)
    grad_k_low = grad_key_own.astype(jnp.bfloat16)
    grad_v_low = grad_value_own.astype(jnp.bfloat16)
    grad_wq = t_times(normed1, grad_q_low)
    grad_wk = t_times(normed1, grad_k_low)
    grad_wv = t_times(normed1, grad_v_low)
    grad_normed1 = times_t(grad_q_low, wq) + times_t(grad_k_low, wk) + times_t(grad_v_low, wv)
    grad_gain_one = jnp.sum(grad_normed1 * scaled1, axis=0)
    grad_tokens = grad_hidden + norm_back(
        grad_normed1, gain_one.astype(jnp.float32), scaled1, inverse1
    )
    part_wq, part_wk, part_wv, part_wo, part_gain_one, part_table = (
        lax.psum_scatter(
            grad_wq.astype(jnp.bfloat16), "wt", scatter_dimension=0, tiled=True
        ).astype(jnp.float32),
        lax.psum_scatter(
            grad_wk.astype(jnp.bfloat16), "wt", scatter_dimension=0, tiled=True
        ).astype(jnp.float32),
        lax.psum_scatter(
            grad_wv.astype(jnp.bfloat16), "wt", scatter_dimension=0, tiled=True
        ).astype(jnp.float32),
        lax.psum_scatter(
            grad_wo.astype(jnp.bfloat16), "wt", scatter_dimension=0, tiled=True
        ).astype(jnp.float32),
        lax.psum_scatter(
            grad_gain_one.astype(jnp.bfloat16), "wt", scatter_dimension=0, tiled=True
        ).astype(jnp.float32),
        lax.psum_scatter(
            grad_table.astype(jnp.bfloat16), "wt", scatter_dimension=0, tiled=True
        ).astype(jnp.float32),
    )
    sums = (
        lax.psum(part_wq.astype(jnp.bfloat16), ("batch", "ctx")).astype(jnp.float32),
        lax.psum(part_wk.astype(jnp.bfloat16), ("batch", "ctx")).astype(jnp.float32),
        lax.psum(part_wv.astype(jnp.bfloat16), ("batch", "ctx")).astype(jnp.float32),
        lax.psum(part_wo.astype(jnp.bfloat16), ("batch", "ctx")).astype(jnp.float32),
        lax.psum(part_gain_one.astype(jnp.bfloat16), ("batch", "ctx")).astype(jnp.float32),
        lax.psum(part_table.astype(jnp.bfloat16), ("batch", "ctx")).astype(jnp.float32),
        lax.psum(part_first.astype(jnp.bfloat16), ("batch", "ctx")).astype(jnp.float32),
        lax.psum(part_second.astype(jnp.bfloat16), ("batch", "ctx")).astype(jnp.float32),
        lax.psum(part_gain_two.astype(jnp.bfloat16), ("batch", "ctx")).astype(jnp.float32),
    )
    return (
        result.astype(jnp.bfloat16)[None],
        grad_tokens.astype(jnp.bfloat16)[None],
        mem_key_total[None],
        mem_value_total[None],
        sums[4],
        sums[8],
        sums[5],
        sums[0],
        sums[1],
        sums[2],
        sums[3],
        sums[6],
        sums[7],
    )


def solution(mesh):
    in_specs = (
        P(("batch", "wt"), "ctx", None),
        P(("batch", "wt"), None, None),
        P(("batch", "wt"), None, None),
        P("wt"),
        P("wt", None),
        P("wt", None),
        P("wt", None),
        P("wt", None),
        P("wt", None),
        P("wt"),
        P("wt", None),
        P("wt", None),
        P(),
        P(("batch", "wt"), "ctx", None),
    )
    out_specs = (
        P(("batch", "wt"), "ctx", None),
        P(("batch", "wt"), "ctx", None),
        P(("batch", "wt"), None, None),
        P(("batch", "wt"), None, None),
        P("wt"),
        P("wt"),
        P("wt", None),
        P("wt", None),
        P("wt", None),
        P("wt", None),
        P("wt", None),
        P("wt", None),
        P("wt", None),
    )
    return jax.shard_map(shards, mesh=mesh, in_specs=in_specs, out_specs=out_specs, check_vma=False)
```

profile of v0, /device:TPU:0, one launch (start us, length us, event | category | flops | bytes accessed | tf_op | source)
XLA Modules:
  0.0 1362.5 jit_solution(13265489076617069256)
XLA Ops:
  12.1 1.9 all-gather
  14.3 1.8 all_gather.47
  16.8 1.8 all-gather.1
  19.2 2.3 all-gather.9.cloned.1.call-done
  21.5 1.6 convolution_convert_fusion.10
  24.0 9.5 all-gather.11.cloned.1.call-done
  33.5 1.6 convolution_convert_fusion.9
  35.2 19.8 %all_gather.46 = bf16[512,768]{1,0:T(8,128)(2,1)S(1)} all-gather(bf16[128,768]{1,0:T(8,128)(2,1)S(1)} %convolution_convert_fusion.9), channel_id=1, replica_groups=mesh['batch'=4,'ctx'=4,'wt'=2] {'ctx'}, dimensions={0}, use_global_device_ids=true | all-gather | bytes 983040 | tf_op jit(solution)/shard_map/all_gather | solution.py:79
  55.2 1.7 fusion.99
  58.3 283.1 %while.47 = (s32[]{:T(128)}, f32[12,128]{1,0:T(8,128)}, f32[12,128]{1,0:T(8,128)}, s32[2]{0:T(128)S(1)}, bf16[512,768]{0,1:T(8,128)(2,1)S(1)}, /*index=5*/bf16[1...) while((s32[]{:T(128)}, f32[12,128]{1,0:T(8,128)}, ...), condition=%wide.region_6.7_spmd.clone, body=%wide.region_3.6_spmd.clone.sunk | while | flops 78318976 | bytes 12339127 | solution.py:111
  59.8 130.0 %gather_fusion = s32[32768]{0:T(1024)S(1)} fusion(s32[1023]{0:T(1024)S(1)} %get-tuple-element.1205, s32[32768]{0:T(1024)S(1)} %broadcast_clamp_fusion.6), kind=kCustom, calls=%fused_computation.clone.clone.1 | custom fusion | bytes 393216 | tf_op jit(solution)/shard_map/while/body/eval_jaxpr/gather | solution.py:92
  191.3 1.6 copy.222
  195.1 2.0 fusion.182
  201.3 130.0 %gather_fusion = s32[32768]{0:T(1024)S(1)} fusion(s32[1023]{0:T(1024)S(1)} %get-tuple-element.1205, s32[32768]{0:T(1024)S(1)} %broadcast_clamp_fusion.6), kind=kCustom, calls=%fused_computation.clone.clone.1 | custom fusion | bytes 393216 | tf_op jit(solution)/shard_map/while/body/eval_jaxpr/gather | solution.py:92
  332.8 1.6 copy.222
  336.6 2.0 fusion.182
  341.4 1.6 convolution_convert_fusion.8
  343.1 18.4 %all_gather.49 = bf16[512,768]{1,0:T(8,128)(2,1)S(1)} all-gather(bf16[128,768]{1,0:T(8,128)(2,1)S(1)} %convolution_convert_fusion.8), channel_id=1, replica_groups=mesh['batch'=4,'ctx'=4,'wt'=2] {'ctx'}, dimensions={0}, use_global_device_ids=true | all-gather | bytes 983040 | tf_op jit(solution)/shard_map/all_gather | solution.py:80
  362.7 1.7 convolution_bitcast_fusion.2
  364.4 284.0 %while.48 = (s32[]{:T(128)}, f32[128,12,64]{0,2,1:T(8,128)}, s32[2]{0:T(128)S(1)}, bf16[512,768]{0,1:T(8,128)(2,1)}, bf16[512,768]{0,1:T(8,128)(2,1)S(1)}, /*ind...) while((s32[]{:T(128)}, f32[128,12,64]{0,2,1:T(8,128)}, ...), condition=%wide.region_8.9_spmd.clone, body=%wide.region_7.8_spmd.clone.sunk | while | flops 128745856 | bytes 12664803 | solution.py:125
  366.9 2.3 constant_dynamic-slice_fusion.10
  370.1 130.0 %gather_fusion.1 = s32[32768]{0:T(1024)S(1)} fusion(s32[1023]{0:T(1024)S(1)} %get-tuple-element.1245, s32[32768]{0:T(1024)S(1)} %broadcast_clamp_fusion.7), kind=kCustom, calls=%fused_computation.1.clone.clone.1 | custom fusion | bytes 393216 | tf_op jit(solution)/shard_map/while/body/eval_jaxpr/gather | solution.py:92
  501.6 1.6 copy.224
  503.3 3.2 fusion.189
  509.0 2.2 constant_dynamic-slice_fusion.10
  512.1 130.0 %gather_fusion.1 = s32[32768]{0:T(1024)S(1)} fusion(s32[1023]{0:T(1024)S(1)} %get-tuple-element.1245, s32[32768]{0:T(1024)S(1)} %broadcast_clamp_fusion.7), kind=kCustom, calls=%fused_computation.1.clone.clone.1 | custom fusion | bytes 393216 | tf_op jit(solution)/shard_map/while/body/eval_jaxpr/gather | solution.py:92
  643.6 1.6 copy.224
  645.2 3.2 fusion.189
  649.5 1.8 multiply_reduce_fusion.2
  651.4 3.3 fusion.92
  654.7 4.8 fusion.52
  659.6 2.3 multiply_reduce_fusion
  664.6 1.6 fusion.75
  668.4 294.8 %while.49 = (s32[]{:T(128)}, f32[128,12,64]{0,2,1:T(8,128)}, f32[32,12]{0,1:T(8,128)S(1)}, bf16[2,256,768]{2,1,0:T(8,128)(2,1)}, bf16[2,256,768]{2,1,0:T(8,128)(...) while((s32[]{:T(128)}, f32[128,12,64]{0,2,1:T(8,128)}, ...), condition=%wide.region_12.13_spmd.clone, body=%wide.region_11.12_spmd.clone.sunk | while | flops 307135616 | bytes 21652508 | solution.py:214
  672.0 130.0 %gather_fusion.2 = s32[32768]{0:T(1024)S(1)} fusion(s32[1023]{0:T(1024)S(1)} %get-tuple-element.1299, s32[32768]{0:T(1024)S(1)} %broadcast_clamp_fusion.8), kind=kCustom, calls=%fused_computation.2.clone.clone.1 | custom fusion | bytes 393216 | tf_op jit(solution)/shard_map/while/body/eval_jaxpr/gather | solution.py:92
  803.6 1.7 fusion.204
  808.0 2.0 fusion.206
  810.0 1.9 fusion.207
  819.4 130.0 %gather_fusion.2 = s32[32768]{0:T(1024)S(1)} fusion(s32[1023]{0:T(1024)S(1)} %get-tuple-element.1299, s32[32768]{0:T(1024)S(1)} %broadcast_clamp_fusion.8), kind=kCustom, calls=%fused_computation.2.clone.clone.1 | custom fusion | bytes 393216 | tf_op jit(solution)/shard_map/while/body/eval_jaxpr/gather | solution.py:92
  951.0 1.7 fusion.204
  955.3 2.0 fusion.206
  957.3 1.9 fusion.207
  965.2 1.6 convolution_convert_fusion.6
  968.4 17.5 %reduce-scatter.12.cloned.1.call-done = bf16[128,768]{1,0:T(8,128)(2,1)} async-done(((bf16[512,768]{1,0:T(8,128)(2,1)}), bf16[128,768]{1,0:T(8,128)(2,1)}) %reduce-scatter.12.cloned.1.call-update) | async-done | bytes 196624 | tf_op jit(solution)/shard_map/reduce_scatter | solution.py:220
  985.9 2.5 convolution_convert_fusion.5
  988.6 22.8 %reduce-scatter.14.cloned.1.call-done = bf16[128,768]{1,0:T(8,128)(2,1)} async-done(((bf16[512,768]{1,0:T(8,128)(2,1)}), bf16[128,768]{1,0:T(8,128)(2,1)}) %reduce-scatter.14.cloned.1.call-update) | async-done | bytes 196624 | tf_op jit(solution)/shard_map/reduce_scatter | solution.py:223
  1011.4 2.5 convolution_convert_fusion.4
  1014.0 3.7 convolution_convert_fusion.1
  1019.1 3.8 convolution_convert_fusion
  1023.8 11.0 reduce-scatter.22.cloned.1.call-done
  1034.8 12.7 reduce-scatter.18.cloned.1.call-done
  1047.6 12.6 reduce-scatter.20.cloned.1.call-done
  1060.2 16.7 %reduce-scatter.24.cloned.1.call-done = bf16[384,3072]{1,0:T(8,128)(2,1)} async-done(((bf16[768,3072]{1,0:T(8,128)(2,1)}), bf16[384,3072]{1,0:T(8,128)(2,1)}) %reduce-scatter.24.cloned.1.call-update) | async-done | bytes 2359312 | tf_op jit(solution)/shard_map/reduce_scatter | solution.py:161
  1076.9 16.6 %reduce-scatter.26.cloned.1.call-done = bf16[1536,768]{1,0:T(8,128)(2,1)} async-done(((bf16[3072,768]{1,0:T(8,128)(2,1)}), bf16[1536,768]{1,0:T(8,128)(2,1)}) %reduce-scatter.26.cloned.1.call-update) | async-done | bytes 2359312 | tf_op jit(solution)/shard_map/reduce_scatter | solution.py:164
  1098.1 20.5 %all-reduce.4 = (bf16[1,20,768]{2,1,0:T(8,128)(2,1)S(1)}, bf16[1,20,768]{2,1,0:T(8,128)(2,1)S(1)}) all-reduce(bf16[1,20,768]{2,1,0:T(8,128)(2,1)S(1)} %broadcast_in_dim.44, bf16[1,20,768]{2,1,0:T(8,128)(2,1)S(1)} %broadcast_in_dim.55), channel_id=1, replica_groups=mesh['batch'=4,'ctx'=4,'wt'=2] {'ctx'}, use_global_device_ids=true, to_apply=%region_16.17 | all-reduce | flops 30720 | bytes 122880 | tf_op jit(solution)/shard_map/psum | solution.py:228
  1119.9 1.8 fusion.101
  1121.8 4.1 fusion.54
  1126.8 1.8 convolution_add_fusion.1
  1129.3 2.5 all-reduce.5
  1131.9 42.3 %all-reduce.2 = (bf16[16,12]{0,1:T(8,128)(2,1)S(1)}, bf16[384]{0:T(512)(128)(2,1)S(1)}, bf16[384]{0:T(512)(128)(2,1)S(1)}) all-reduce(bf16[16,12]{0,1:T(8,128)(2,1)S(1)} %copy.182, bf16[384]{0:T(512)(128)(2,1)S(1)} %dynamic-slice.1, bf16[384]{0:T(512)(128)(2,1)S(1)} %dynamic-slice.3), channel_id=1, replica_groups=mesh['batch'=4,'ctx'=4,'wt'=2] {'batch','ctx'}, use_global_device_ids=true, to_apply=%region_25.26 | all-reduce | flops 960 | bytes 3840 | tf_op jit(solution)/shard_map/psum | solution.py:268
  1176.9 168.2 %all-reduce.8.cloned.1.call-done = (bf16[384,768]{1,0:T(8,128)(2,1)}, bf16[384,768]{1,0:T(8,128)(2,1)}, bf16[384,768]{1,0:T(8,128)(2,1)}, bf16[384,768]{1,0:T(8,...) async-done(((bf16[384,768]{1,0:T(8,128)(2,1)}, bf16[384,768]{1,0:T(8,128)(2,1)}, bf16[384,768]{1,0:T(8,128)(2,1)}, bf16[384,768]{1,0:T(8,128)(2,1)}, ...) | async-done | bytes 7077904 | tf_op jit(solution)/shard_map/psum | solution.py:263
  1345.1 2.2 convert_element_type.257
  1350.6 2.8 convert_element_type.265
  1353.4 2.5 convert_element_type.267
  (286 shorter events, 71.5 us)
Async XLA Ops:
  7.2 14.3 %all-gather.9.cloned.1.call-start = ((), (), s32[]{:S(2)}) async-start(), calls=%async_computation.9 | async-start | bytes 1769472 | tf_op jit(solution)/shard_map/all_gather | solution.py:53
  7.9 25.6 %all-gather.11.cloned.1.call-start = ((), (), s32[]{:S(2)}) async-start(), calls=%async_computation.10 | async-start | bytes 1769472 | tf_op jit(solution)/shard_map/all_gather | solution.py:54
  8.7 332.8 %all-gather.13.cloned.1.call-start = ((), (), s32[]{:S(2)}) async-start(), calls=%async_computation.11 | async-start | bytes 1769472 | tf_op jit(solution)/shard_map/all_gather | solution.py:55
  9.4 640.1 %all-gather.15.cloned.1.call-start = ((), (), s32[]{:S(2)}) async-start(), calls=%async_computation.12 | async-start | bytes 1769472 | tf_op jit(solution)/shard_map/all_gather | solution.py:56
  10.0 641.4 %all-gather.17.cloned.1.call-start = ((), (), s32[]{:S(2)}) async-start(), calls=%async_computation.13 | async-start | bytes 7077888 | tf_op jit(solution)/shard_map/all_gather | solution.py:61
  10.6 3.4 copy-start.1
  10.6 3.6 copy-start.46
  10.6 3.7 copy-start.54
  10.6 6.2 copy-start.56
  10.6 644.0 %all-gather.19.cloned.1.call-start = ((), (), s32[]{:S(2)}) async-start(), calls=%async_computation.14 | async-start | bytes 7077888 | tf_op jit(solution)/shard_map/all_gather | solution.py:62
  11.2 974.7 %reduce-scatter.12.cloned.1.call-start = ((), (), s32[]{:S(2)}) async-start(), calls=%async_computation.15 | async-start | bytes 983040 | tf_op jit(solution)/shard_map/reduce_scatter | solution.py:220
  14.0 21.1 %copy-start.36 = (f32[768]{0:T(1024)}, f32[768]{0:T(1024)S(1)}, u32[]{:S(2)}) copy-start(f32[768]{0:T(1024)S(1)} %reshape.355) | copy-start | bytes 9220
  14.2 21.0 %copy-start.47 = (f32[128]{0:T(128)}, f32[128]{0:T(128)S(1)}, u32[]{:S(2)}) copy-start(f32[128]{0:T(128)S(1)} %add_rsqrt_fusion.1) | copy-start | bytes 1540
  14.3 40.9 %copy-start.27 = (bf16[20,12,64]{2,1,0:T(8,128)(2,1)}, bf16[20,12,64]{2,1,0:T(8,128)(2,1)S(1)}, u32[]{:S(2)}) copy-start(bf16[20,12,64]{2,1,0:T(8,128)(2,1)S(1)} %reshape_squeeze.6) | copy-start | bytes 92164
  35.1 23.1 %copy-start = (s32[1023]{0:T(1024)S(1)}, s32[1023]{0:T(1024)}, u32[]{:S(2)}) copy-start(s32[1023]{0:T(1024)} %param.32) | copy-start | bytes 12280
  58.3 283.1 %copy-start.2 = (bf16[1,128,768]{2,1,0:T(8,128)(2,1)S(1)}, bf16[1,128,768]{2,1,0:T(8,128)(2,1)}, u32[]{:S(2)}) copy-start(bf16[1,128,768]{2,1,0:T(8,128)(2,1)} %param.20) | copy-start | bytes 589828
  58.3 283.1 %copy-start.37 = (f32[768]{0:T(1024)S(1)}, f32[768]{0:T(1024)}, u32[]{:S(2)}) copy-start(f32[768]{0:T(1024)} %copy-done.36) | copy-start | bytes 9220
  58.3 283.1 %copy-start.48 = (f32[128]{0:T(128)S(1)}, f32[128]{0:T(128)}, u32[]{:S(2)}) copy-start(f32[128]{0:T(128)} %copy-done.47) | copy-start | bytes 1540
  343.1 19.6 %copy-start.33 = (f32[12,128,20]{1,2,0:T(8,128)S(1)}, f32[12,128,20]{1,2,0:T(8,128)}, u32[]{:S(2)}) copy-start(f32[12,128,20]{1,2,0:T(8,128)} %copy-done.32) | copy-start | bytes 368644
  343.1 19.6 %copy-start.43 = (bf16[20,12,64]{2,1,0:T(8,128)(2,1)S(1)}, bf16[20,12,64]{2,1,0:T(8,128)(2,1)}, u32[]{:S(2)}) copy-start(bf16[20,12,64]{2,1,0:T(8,128)(2,1)} %reshape_squeeze.7) | copy-start | bytes 92164
  364.4 285.1 %copy-start.3 = (bf16[1,128,768]{2,1,0:T(8,128)(2,1)S(1)}, bf16[1,128,768]{2,1,0:T(8,128)(2,1)}, u32[]{:S(2)}) copy-start(bf16[1,128,768]{2,1,0:T(8,128)(2,1)} %param.20) | copy-start | bytes 589828
  501.6 1.6 copy-start.11
  643.6 1.6 copy-start.11
  648.4 2.9 copy-start.41
  649.5 1.9 copy-start.20
  651.3 10.6 copy-start.7
  651.3 10.6 copy-start.50
  651.4 3.3 copy-start.25
  654.6 4.9 copy-start.9
  654.7 4.9 copy-start.5
  659.6 2.3 copy-start.16
  661.9 2.8 copy-start.22
  663.3 3.0 copy-start.34
  663.3 3.0 copy-start.44
  663.3 4.1 copy-start.28
  663.8 4.6 copy-start.53
  963.2 1.9 copy-start.4
  963.2 1.9 copy-start.38
  963.2 2.0 copy-start.49
  963.3 48.2 %reduce-scatter.14.cloned.1.call-start = ((), (), s32[]{:S(2)}) async-start(), calls=%async_computation.16 | async-start | bytes 983040 | tf_op jit(solution)/shard_map/reduce_scatter | solution.py:223
  964.0 59.8 %reduce-scatter.16.cloned.1.call-start = ((), (), s32[]{:S(2)}) async-start(), calls=%async_computation.17 | async-start | bytes 1769472 | tf_op jit(solution)/shard_map/reduce_scatter | solution.py:243
  964.1 2.8 copy-start.13
  964.1 2.8 copy-start.21
  966.8 68.0 %reduce-scatter.22.cloned.1.call-start = ((), (), s32[]{:S(2)}) async-start(), calls=%async_computation.20 | async-start | bytes 1769472 | tf_op jit(solution)/shard_map/reduce_scatter | solution.py:252
  968.4 79.2 %reduce-scatter.18.cloned.1.call-start = ((), (), s32[]{:S(2)}) async-start(), calls=%async_computation.18 | async-start | bytes 1769472 | tf_op jit(solution)/shard_map/reduce_scatter | solution.py:246
  988.5 25.5 %copy-start.8 = (f32[128,768]{1,0:T(8,128)S(1)}, f32[128,768]{1,0:T(8,128)}, u32[]{:S(2)}) copy-start(f32[128,768]{1,0:T(8,128)} %copy-done.7) | copy-start | bytes 1179652
  988.5 25.5 %copy-start.17 = (bf16[128,3072]{1,0:T(8,128)(2,1)S(1)}, bf16[128,3072]{1,0:T(8,128)(2,1)}, u32[]{:S(2)}) copy-start(bf16[128,3072]{1,0:T(8,128)(2,1)} %copy-done.16) | copy-start | bytes 2359300
  988.5 25.5 %copy-start.42 = (f32[768]{0:T(1024)S(1)}, f32[768]{0:T(1024)}, u32[]{:S(2)}) copy-start(f32[768]{0:T(1024)} %reshape.356) | copy-start | bytes 9220
  988.5 25.5 %copy-start.51 = (f32[128]{0:T(128)S(1)}, f32[128]{0:T(128)}, u32[]{:S(2)}) copy-start(f32[128]{0:T(128)} %copy-done.50) | copy-start | bytes 1540
  988.5 71.7 %reduce-scatter.20.cloned.1.call-start = ((), (), s32[]{:S(2)}) async-start(), calls=%async_computation.19 | async-start | bytes 1769472 | tf_op jit(solution)/shard_map/reduce_scatter | solution.py:249
  1014.0 63.0 %reduce-scatter.24.cloned.1.call-start = ((), (), s32[]{:S(2)}) async-start(), calls=%async_computation.21 | async-start | bytes 7077888 | tf_op jit(solution)/shard_map/reduce_scatter | solution.py:161
  1017.7 75.8 %reduce-scatter.26.cloned.1.call-start = ((), (), s32[]{:S(2)}) async-start(), calls=%async_computation.22 | async-start | bytes 7077888 | tf_op jit(solution)/shard_map/reduce_scatter | solution.py:164
  1023.0 102.9 %reduce-scatter.28.cloned.1.call-start = ((), (), s32[]{:S(2)}) async-start(), calls=%async_computation.23 | async-start | bytes 12288
  1023.7 321.3 %all-reduce.8.cloned.1.call-start = ((), (), s32[]{:S(2)}) async-start(), calls=%async_computation.24 | async-start | bytes 14155776 | tf_op jit(solution)/shard_map/psum | solution.py:263
  1093.6 1.9 copy-start.40
  1093.6 3.2 copy-start.35
  1121.7 5.0 copy-start.23
  1125.9 2.7 copy-start.14
  1125.9 2.7 copy-start.24
  1345.1 2.3 copy-start.31
  1345.1 3.3 copy-start.30
  1347.4 2.2 copy-start.29
  1348.4 2.2 copy-start.19
  1350.6 2.8 copy-start.18
  (12 other events, 13.8 us)
Sparse Core Ops, SparseCore 0:
  9.6 11.9 all-gather.8
  23.1 10.3 all-gather.10
  35.0 10.3 all-gather.12
  46.9 10.3 all-gather.14
  58.7 15.5 all-gather.16
  75.7 15.6 all-gather.18
  963.4 22.5 reduce-scatter.11
  988.8 22.5 reduce-scatter.13
  1014.2 7.9 reduce-scatter.15
  1025.0 9.8 reduce-scatter.21
  1037.7 9.8 reduce-scatter.17
  1050.3 9.8 reduce-scatter.19
  1063.1 13.7 reduce-scatter.23
  1079.7 13.7 reduce-scatter.25
  1095.6 8.5 reduce-scatter.27
  1110.5 234.5 all-reduce.7
where the time goes:
time: 1360 us
  local copies, waits for them, and re-layouts  816 us (60%)
  waiting for transfers between devices  295 us (22%)
  blocking collectives  109 us (8%)
  matrix products  87.6 us (6%)
  other arithmetic  27.3 us (2%)
  between operations  15.4 us (1%)
    gather x14, local copies, waits for them, and re-layouts, scores_at(): bucket_ids = buckets[where]  781 us
    psum x1, waiting for transfers between devices, shards(): lax.psum(part_wq.astype(jnp.bfloat16), ('batch', 'ctx')).astype(jnp.float32)  168 us
    psum x1, blocking collectives, shards(): lax.psum(part_table.astype(jnp.bfloat16), ('batch', 'ctx'))  42.3 us
  transfers between devices with their start and end apart: 16, of which 10 were waited for; matrix products, arithmetic and copies ran while one was open for 45% of the time, Pallas kernels for 0%

commit v1 on v0

--- a/solution.py
+++ b/solution.py
@@ -2,6 +2,7 @@
 import jax.numpy as jnp
 from jax import lax
 from jax.sharding import PartitionSpec as P
+from jax.lax import psum
 
 KB = 256
 EPS = 1e-06
@@ -260,7 +261,7 @@
         ).astype(jnp.float32),
     )
     sums = (
-        lax.psum(part_wq.astype(jnp.bfloat16), ("batch", "ctx")).astype(jnp.float32),
+        psum(psum(part_wq.astype(jnp.bfloat16), "ctx"), "batch").astype(jnp.float32),
         lax.psum(part_wk.astype(jnp.bfloat16), ("batch", "ctx")).astype(jnp.float32),
         lax.psum(part_wv.astype(jnp.bfloat16), ("batch", "ctx")).astype(jnp.float32),
         lax.psum(part_wo.astype(jnp.bfloat16), ("batch", "ctx")).astype(jnp.float32),

time: 1360 us -> 1450 us (1.066)
  waiting for transfers between devices: 295 us -> 375 us
    psum x1 -> x3, waiting for transfers between devices: 168 us -> 233 us  [the longest x1 205 us: shards(): lax.psum(part_wk.astype(jnp.bfloat16), ('batch', 'ctx')).astype(jnp.float32)]
  transfers between devices with their start and end apart: 16 -> 18, of which waited for: 10 -> 12; matrix products, arithmetic and copies ran while one was open for 45% -> 42% of each run, Pallas kernels for 0% -> 0%
where the time goes in v1:
time: 1450 us; the launch traced here: 1440 us
  local copies, waits for them, and re-layouts  817 us (56%)
  waiting for transfers between devices  375 us (26%)
  blocking collectives  106 us (7%)
  matrix products  89.7 us (6%)
  other arithmetic  28.4 us (2%)
  between operations  15.7 us (1%)
    gather x14, local copies, waits for them, and re-layouts, scores_at(): bucket_ids = buckets[where]  781 us
    psum x1, waiting for transfers between devices, shards(): lax.psum(part_wk.astype(jnp.bfloat16), ('batch', 'ctx')).astype(jnp.float32)  205 us
    psum x1, blocking collectives, shards(): lax.psum(part_table.astype(jnp.bfloat16), ('batch', 'ctx'))  39.3 us
  transfers between devices with their start and end apart: 18, of which 12 were waited for; matrix products, arithmetic and copies ran while one was open for 42% of the time, Pallas kernels for 0%

profile of v1, /device:TPU:0, one launch (start us, length us, event | category | flops | bytes accessed | tf_op | source)
XLA Modules:
  0.0 1444.6 jit_solution(11390016859340149961)
XLA Ops:
  12.1 1.9 all-gather
  14.3 1.8 all_gather.47
  16.8 1.8 all-gather.1
  19.2 2.3 all-gather.9.cloned.1.call-done
  24.0 9.5 all-gather.11.cloned.1.call-done
  35.2 19.8 %all_gather.46 = bf16[512,768]{1,0:T(8,128)(2,1)S(1)} all-gather(bf16[128,768]{1,0:T(8,128)(2,1)S(1)} %convolution_convert_fusion.9), channel_id=1, replica_groups=mesh['batch'=4,'ctx'=4,'wt'=2] {'ctx'}, dimensions={0}, use_global_device_ids=true | all-gather | bytes 983040 | tf_op jit(solution)/shard_map/all_gather | solution.py:80
  55.2 1.7 fusion.99
  58.3 283.1 %while.47 = (s32[]{:T(128)}, f32[12,128]{1,0:T(8,128)}, f32[12,128]{1,0:T(8,128)}, s32[2]{0:T(128)S(1)}, bf16[512,768]{0,1:T(8,128)(2,1)S(1)}, /*index=5*/bf16[1...) while((s32[]{:T(128)}, f32[12,128]{1,0:T(8,128)}, ...), condition=%wide.region_6.7_spmd.clone, body=%wide.region_3.6_spmd.clone.sunk | while | flops 78318976 | bytes 12339127 | solution.py:112
  59.8 130.0 %gather_fusion = s32[32768]{0:T(1024)S(1)} fusion(s32[1023]{0:T(1024)S(1)} %get-tuple-element.1204, s32[32768]{0:T(1024)S(1)} %broadcast_clamp_fusion.6), kind=kCustom, calls=%fused_computation.clone.clone.1 | custom fusion | bytes 393216 | tf_op jit(solution)/shard_map/while/body/eval_jaxpr/gather | solution.py:93
  191.3 1.6 copy.222
  195.1 2.0 fusion.182
  201.3 130.0 %gather_fusion = s32[32768]{0:T(1024)S(1)} fusion(s32[1023]{0:T(1024)S(1)} %get-tuple-element.1204, s32[32768]{0:T(1024)S(1)} %broadcast_clamp_fusion.6), kind=kCustom, calls=%fused_computation.clone.clone.1 | custom fusion | bytes 393216 | tf_op jit(solution)/shard_map/while/body/eval_jaxpr/gather | solution.py:93
  332.8 1.6 copy.222
  336.6 2.0 fusion.182
  341.4 1.6 convolution_convert_fusion.8
  343.1 18.5 %all_gather.49 = bf16[512,768]{1,0:T(8,128)(2,1)S(1)} all-gather(bf16[128,768]{1,0:T(8,128)(2,1)S(1)} %convolution_convert_fusion.8), channel_id=1, replica_groups=mesh['batch'=4,'ctx'=4,'wt'=2] {'ctx'}, dimensions={0}, use_global_device_ids=true | all-gather | bytes 983040 | tf_op jit(solution)/shard_map/all_gather | solution.py:81
  362.7 1.7 convolution_bitcast_fusion.2
  364.4 284.0 %while.48 = (s32[]{:T(128)}, f32[128,12,64]{0,2,1:T(8,128)}, s32[2]{0:T(128)S(1)}, bf16[512,768]{0,1:T(8,128)(2,1)}, bf16[512,768]{0,1:T(8,128)(2,1)S(1)}, /*ind...) while((s32[]{:T(128)}, f32[128,12,64]{0,2,1:T(8,128)}, ...), condition=%wide.region_8.9_spmd.clone, body=%wide.region_7.8_spmd.clone.sunk | while | flops 128745856 | bytes 12664803 | solution.py:126
  367.0 2.3 constant_dynamic-slice_fusion.10
  370.1 130.0 %gather_fusion.1 = s32[32768]{0:T(1024)S(1)} fusion(s32[1023]{0:T(1024)S(1)} %get-tuple-element.1244, s32[32768]{0:T(1024)S(1)} %broadcast_clamp_fusion.7), kind=kCustom, calls=%fused_computation.1.clone.clone.1 | custom fusion | bytes 393216 | tf_op jit(solution)/shard_map/while/body/eval_jaxpr/gather | solution.py:93
  501.6 1.6 copy.224
  503.3 3.2 fusion.189
  509.0 2.2 constant_dynamic-slice_fusion.10
  512.1 130.0 %gather_fusion.1 = s32[32768]{0:T(1024)S(1)} fusion(s32[1023]{0:T(1024)S(1)} %get-tuple-element.1244, s32[32768]{0:T(1024)S(1)} %broadcast_clamp_fusion.7), kind=kCustom, calls=%fused_computation.1.clone.clone.1 | custom fusion | bytes 393216 | tf_op jit(solution)/shard_map/while/body/eval_jaxpr/gather | solution.py:93
  643.6 1.6 copy.224
  645.2 3.2 fusion.189
  649.5 1.8 multiply_reduce_fusion.2
  651.4 3.3 fusion.92
  654.7 4.9 fusion.52
  659.6 2.3 multiply_reduce_fusion
  668.4 296.4 %while.49 = (s32[]{:T(128)}, f32[128,12,64]{0,2,1:T(8,128)}, f32[32,12]{0,1:T(8,128)}, bf16[2,256,768]{2,1,0:T(8,128)(2,1)}, bf16[2,256,768]{2,1,0:T(8,128)(2,1)...) while((s32[]{:T(128)}, f32[128,12,64]{0,2,1:T(8,128)}, ...), condition=%wide.region_12.13_spmd.clone, body=%wide.region_11.12_spmd.clone.sunk | while | flops 307135616 | bytes 21652508 | solution.py:215
  672.2 130.0 %gather_fusion.2 = s32[32768]{0:T(1024)S(1)} fusion(s32[1023]{0:T(1024)S(1)} %get-tuple-element.1298, s32[32768]{0:T(1024)S(1)} %broadcast_clamp_fusion.8), kind=kCustom, calls=%fused_computation.2.clone.clone.1 | custom fusion | bytes 393216 | tf_op jit(solution)/shard_map/while/body/eval_jaxpr/gather | solution.py:93
  803.8 1.8 fusion.204
  808.2 2.0 fusion.206
  810.2 2.5 fusion.207
  820.4 130.0 %gather_fusion.2 = s32[32768]{0:T(1024)S(1)} fusion(s32[1023]{0:T(1024)S(1)} %get-tuple-element.1298, s32[32768]{0:T(1024)S(1)} %broadcast_clamp_fusion.8), kind=kCustom, calls=%fused_computation.2.clone.clone.1 | custom fusion | bytes 393216 | tf_op jit(solution)/shard_map/while/body/eval_jaxpr/gather | solution.py:93
  952.0 1.8 fusion.204
  956.4 2.0 fusion.206
  958.4 2.5 fusion.207
  965.9 2.5 convolution_convert_fusion.6
  970.0 6.7 reduce-scatter.16.cloned.1.call-done
  978.3 25.8 %reduce-scatter.12.cloned.1.call-done = bf16[128,768]{1,0:T(8,128)(2,1)} async-done(((bf16[512,768]{1,0:T(8,128)(2,1)}), bf16[128,768]{1,0:T(8,128)(2,1)}) %reduce-scatter.12.cloned.1.call-update) | async-done | bytes 196624 | tf_op jit(solution)/shard_map/reduce_scatter | solution.py:221
  1004.1 2.5 convolution_convert_fusion.5
  1006.7 23.0 %reduce-scatter.14.cloned.1.call-done = bf16[128,768]{1,0:T(8,128)(2,1)} async-done(((bf16[512,768]{1,0:T(8,128)(2,1)}), bf16[128,768]{1,0:T(8,128)(2,1)}) %reduce-scatter.14.cloned.1.call-update) | async-done | bytes 196624 | tf_op jit(solution)/shard_map/reduce_scatter | solution.py:224
  1029.7 2.5 convolution_convert_fusion.4
  1032.3 3.7 convolution_convert_fusion.1
  1037.5 3.8 convolution_convert_fusion
  1042.8 27.7 %all-reduce.10.cloned.1.call-done = bf16[384,768]{1,0:T(8,128)(2,1)} async-done(((bf16[384,768]{1,0:T(8,128)(2,1)}), bf16[384,768]{1,0:T(8,128)(2,1)}) %all-reduce.10.cloned.1.call-update) | async-done | bytes 589840 | tf_op jit(solution)/shard_map/psum | solution.py:264
  1070.5 11.2 reduce-scatter.22.cloned.1.call-done
  1081.7 12.5 reduce-scatter.18.cloned.1.call-done
  1094.3 12.8 reduce-scatter.20.cloned.1.call-done
  1107.1 16.6 %reduce-scatter.24.cloned.1.call-done = bf16[384,3072]{1,0:T(8,128)(2,1)} async-done(((bf16[768,3072]{1,0:T(8,128)(2,1)}), bf16[384,3072]{1,0:T(8,128)(2,1)}) %reduce-scatter.24.cloned.1.call-update) | async-done | bytes 2359312 | tf_op jit(solution)/shard_map/reduce_scatter | solution.py:162
  1123.7 16.6 %reduce-scatter.26.cloned.1.call-done = bf16[1536,768]{1,0:T(8,128)(2,1)} async-done(((bf16[3072,768]{1,0:T(8,128)(2,1)}), bf16[1536,768]{1,0:T(8,128)(2,1)}) %reduce-scatter.26.cloned.1.call-update) | async-done | bytes 2359312 | tf_op jit(solution)/shard_map/reduce_scatter | solution.py:165
  1144.8 20.5 %all-reduce.4 = (bf16[1,20,768]{2,1,0:T(8,128)(2,1)S(1)}, bf16[1,20,768]{2,1,0:T(8,128)(2,1)S(1)}) all-reduce(bf16[1,20,768]{2,1,0:T(8,128)(2,1)S(1)} %broadcast_in_dim.44, bf16[1,20,768]{2,1,0:T(8,128)(2,1)S(1)} %broadcast_in_dim.55), channel_id=1, replica_groups=mesh['batch'=4,'ctx'=4,'wt'=2] {'ctx'}, use_global_device_ids=true, to_apply=%region_16.17 | all-reduce | flops 30720 | bytes 122880 | tf_op jit(solution)/shard_map/psum | solution.py:229
  1166.7 1.8 fusion.101
  1168.5 4.1 fusion.54
  1173.5 1.8 convolution_add_fusion.1
  1176.0 2.5 all-reduce.5
  1178.6 39.3 %all-reduce.2 = (bf16[16,12]{0,1:T(8,128)(2,1)S(1)}, bf16[384]{0:T(512)(128)(2,1)S(1)}, bf16[384]{0:T(512)(128)(2,1)S(1)}) all-reduce(bf16[16,12]{0,1:T(8,128)(2,1)S(1)} %copy.182, bf16[384]{0:T(512)(128)(2,1)S(1)} %dynamic-slice.1, bf16[384]{0:T(512)(128)(2,1)S(1)} %dynamic-slice.3), channel_id=1, replica_groups=mesh['batch'=4,'ctx'=4,'wt'=2] {'batch','ctx'}, use_global_device_ids=true, to_apply=%region_25.26 | all-reduce | flops 960 | bytes 3840 | tf_op jit(solution)/shard_map/psum | solution.py:269
  1220.6 2.2 convert_element_type.257
  1222.8 205.2 %all-reduce.14.cloned.1.call-done = (bf16[384,768]{1,0:T(8,128)(2,1)}, bf16[384,768]{1,0:T(8,128)(2,1)}, bf16[384,768]{1,0:T(8,128)(2,1)}, bf16[384,3072]{1,0:T(8,128)(2,1)}, bf16[1536,768]{1,0:T(8,128)(2,1)}) async-done(((bf16[384,768]{1,0:T(8,128)(2,1)}, bf16[384,768]{1,0:T(8,128)(2,1)}, bf16[384,768]{1,0:T(8,128)(2,1)}, bf16[384,3072]{1,0:T(8,128)(2,1)}, bf16[1536,768]{1,0:T(8,128)(2,1)}), ...) | async-done | bytes 6488080 | tf_op jit(solution)/shard_map/psum | solution.py:265
  1428.0 2.2 convert_element_type.259
  1432.5 2.8 convert_element_type.265
  1435.2 2.5 convert_element_type.267
  (290 shorter events, 76.7 us)
Async XLA Ops:
  7.2 14.3 all-gather.9.cloned.1.call-start
  7.9 25.6 %all-gather.11.cloned.1.call-start = ((), (), s32[]{:S(2)}) async-start(), calls=%async_computation.10 | async-start | bytes 1769472 | tf_op jit(solution)/shard_map/all_gather | solution.py:55
  8.7 332.7 %all-gather.13.cloned.1.call-start = ((), (), s32[]{:S(2)}) async-start(), calls=%async_computation.11 | async-start | bytes 1769472 | tf_op jit(solution)/shard_map/all_gather | solution.py:56
  9.4 640.1 %all-gather.15.cloned.1.call-start = ((), (), s32[]{:S(2)}) async-start(), calls=%async_computation.12 | async-start | bytes 1769472 | tf_op jit(solution)/shard_map/all_gather | solution.py:57
  10.0 641.4 %all-gather.17.cloned.1.call-start = ((), (), s32[]{:S(2)}) async-start(), calls=%async_computation.13 | async-start | bytes 7077888 | tf_op jit(solution)/shard_map/all_gather | solution.py:62
  10.6 3.5 copy-start.1
  10.6 3.6 copy-start.45
  10.6 3.7 copy-start.53
  10.6 6.2 copy-start.55
  10.6 644.1 %all-gather.19.cloned.1.call-start = ((), (), s32[]{:S(2)}) async-start(), calls=%async_computation.14 | async-start | bytes 7077888 | tf_op jit(solution)/shard_map/all_gather | solution.py:63
  11.2 965.4 %reduce-scatter.16.cloned.1.call-start = ((), (), s32[]{:S(2)}) async-start(), calls=%async_computation.17 | async-start | bytes 1769472 | tf_op jit(solution)/shard_map/reduce_scatter | solution.py:244
  14.0 21.1 %copy-start.35 = (f32[768]{0:T(1024)}, f32[768]{0:T(1024)S(1)}, u32[]{:S(2)}) copy-start(f32[768]{0:T(1024)S(1)} %reshape.355) | copy-start | bytes 9220
  14.2 20.9 %copy-start.46 = (f32[128]{0:T(128)}, f32[128]{0:T(128)S(1)}, u32[]{:S(2)}) copy-start(f32[128]{0:T(128)S(1)} %add_rsqrt_fusion.1) | copy-start | bytes 1540
  14.3 40.9 %copy-start.27 = (bf16[20,12,64]{2,1,0:T(8,128)(2,1)}, bf16[20,12,64]{2,1,0:T(8,128)(2,1)S(1)}, u32[]{:S(2)}) copy-start(bf16[20,12,64]{2,1,0:T(8,128)(2,1)S(1)} %reshape_squeeze.6) | copy-start | bytes 92164
  35.1 23.1 %copy-start = (s32[1023]{0:T(1024)S(1)}, s32[1023]{0:T(1024)}, u32[]{:S(2)}) copy-start(s32[1023]{0:T(1024)} %param.32) | copy-start | bytes 12280
  58.3 283.1 %copy-start.2 = (bf16[1,128,768]{2,1,0:T(8,128)(2,1)S(1)}, bf16[1,128,768]{2,1,0:T(8,128)(2,1)}, u32[]{:S(2)}) copy-start(bf16[1,128,768]{2,1,0:T(8,128)(2,1)} %param.20) | copy-start | bytes 589828
  58.3 283.1 %copy-start.36 = (f32[768]{0:T(1024)S(1)}, f32[768]{0:T(1024)}, u32[]{:S(2)}) copy-start(f32[768]{0:T(1024)} %copy-done.35) | copy-start | bytes 9220
  58.3 283.1 %copy-start.47 = (f32[128]{0:T(128)S(1)}, f32[128]{0:T(128)}, u32[]{:S(2)}) copy-start(f32[128]{0:T(128)} %copy-done.46) | copy-start | bytes 1540
  343.1 19.6 %copy-start.32 = (f32[12,128,20]{1,2,0:T(8,128)S(1)}, f32[12,128,20]{1,2,0:T(8,128)}, u32[]{:S(2)}) copy-start(f32[12,128,20]{1,2,0:T(8,128)} %copy-done.31) | copy-start | bytes 368644
  343.1 19.6 %copy-start.42 = (bf16[20,12,64]{2,1,0:T(8,128)(2,1)S(1)}, bf16[20,12,64]{2,1,0:T(8,128)(2,1)}, u32[]{:S(2)}) copy-start(bf16[20,12,64]{2,1,0:T(8,128)(2,1)} %reshape_squeeze.7) | copy-start | bytes 92164
  364.4 285.1 %copy-start.3 = (bf16[1,128,768]{2,1,0:T(8,128)(2,1)S(1)}, bf16[1,128,768]{2,1,0:T(8,128)(2,1)}, u32[]{:S(2)}) copy-start(bf16[1,128,768]{2,1,0:T(8,128)(2,1)} %param.20) | copy-start | bytes 589828
  501.6 1.6 copy-start.11
  643.6 1.6 copy-start.11
  648.4 2.9 copy-start.40
  649.5 1.9 copy-start.20
  651.3 10.6 copy-start.7
  651.3 10.6 copy-start.49
  651.4 3.3 copy-start.25
  654.6 4.9 copy-start.9
  654.7 4.9 copy-start.5
  659.6 2.3 copy-start.16
  661.9 2.8 copy-start.22
  663.3 3.0 copy-start.33
  663.3 3.0 copy-start.43
  663.3 4.1 copy-start.28
  668.4 297.5 %copy-start.37 = (f32[768]{0:T(1024)S(1)}, f32[768]{0:T(1024)}, u32[]{:S(2)}) copy-start(f32[768]{0:T(1024)} %copy-done.35) | copy-start | bytes 9220
  668.4 297.5 %copy-start.48 = (f32[128]{0:T(128)S(1)}, f32[128]{0:T(128)}, u32[]{:S(2)}) copy-start(f32[128]{0:T(128)} %copy-done.46) | copy-start | bytes 1540
  968.4 8.3 copy-start.13
  968.4 8.3 copy-start.21
  968.4 35.7 %reduce-scatter.12.cloned.1.call-start = ((), (), s32[]{:S(2)}) async-start(), calls=%async_computation.15 | async-start | bytes 983040 | tf_op jit(solution)/shard_map/reduce_scatter | solution.py:221
  969.2 60.5 %reduce-scatter.14.cloned.1.call-start = ((), (), s32[]{:S(2)}) async-start(), calls=%async_computation.16 | async-start | bytes 983040 | tf_op jit(solution)/shard_map/reduce_scatter | solution.py:224
  969.9 100.5 %all-reduce.10.cloned.1.call-start = ((), (), s32[]{:S(2)}) async-start(), calls=%async_computation.18 | async-start | bytes 1179648 | tf_op jit(solution)/shard_map/psum | solution.py:264
  976.7 27.5 %copy-start.4 = (bf16[1,128,768]{2,1,0:T(8,128)(2,1)S(1)}, bf16[1,128,768]{2,1,0:T(8,128)(2,1)}, u32[]{:S(2)}) copy-start(bf16[1,128,768]{2,1,0:T(8,128)(2,1)} %param.20) | copy-start | bytes 589828
  976.7 105.1 %reduce-scatter.22.cloned.1.call-start = ((), (), s32[]{:S(2)}) async-start(), calls=%async_computation.22 | async-start | bytes 1769472 | tf_op jit(solution)/shard_map/reduce_scatter | solution.py:253
  978.2 116.0 %reduce-scatter.18.cloned.1.call-start = ((), (), s32[]{:S(2)}) async-start(), calls=%async_computation.20 | async-start | bytes 1769472 | tf_op jit(solution)/shard_map/reduce_scatter | solution.py:247
  1006.7 25.7 %copy-start.8 = (f32[128,768]{1,0:T(8,128)S(1)}, f32[128,768]{1,0:T(8,128)}, u32[]{:S(2)}) copy-start(f32[128,768]{1,0:T(8,128)} %copy-done.7) | copy-start | bytes 1179652
  1006.7 25.7 %copy-start.17 = (bf16[128,3072]{1,0:T(8,128)(2,1)S(1)}, bf16[128,3072]{1,0:T(8,128)(2,1)}, u32[]{:S(2)}) copy-start(bf16[128,3072]{1,0:T(8,128)(2,1)} %copy-done.16) | copy-start | bytes 2359300
  1006.7 25.7 %copy-start.41 = (f32[768]{0:T(1024)S(1)}, f32[768]{0:T(1024)}, u32[]{:S(2)}) copy-start(f32[768]{0:T(1024)} %reshape.356) | copy-start | bytes 9220
  1006.7 25.7 %copy-start.50 = (f32[128]{0:T(128)S(1)}, f32[128]{0:T(128)}, u32[]{:S(2)}) copy-start(f32[128]{0:T(128)} %copy-done.49) | copy-start | bytes 1540
  1006.7 100.4 %reduce-scatter.20.cloned.1.call-start = ((), (), s32[]{:S(2)}) async-start(), calls=%async_computation.21 | async-start | bytes 1769472 | tf_op jit(solution)/shard_map/reduce_scatter | solution.py:250
  1032.3 91.4 %reduce-scatter.24.cloned.1.call-start = ((), (), s32[]{:S(2)}) async-start(), calls=%async_computation.23 | async-start | bytes 7077888 | tf_op jit(solution)/shard_map/reduce_scatter | solution.py:162
  1036.1 104.2 %reduce-scatter.26.cloned.1.call-start = ((), (), s32[]{:S(2)}) async-start(), calls=%async_computation.24 | async-start | bytes 7077888 | tf_op jit(solution)/shard_map/reduce_scatter | solution.py:165
  1041.3 131.3 %reduce-scatter.28.cloned.1.call-start = ((), (), s32[]{:S(2)}) async-start(), calls=%async_computation.25 | async-start | bytes 12288
  1042.7 177.9 %all-reduce.12.cloned.1.call-start = ((), (), s32[]{:S(2)}) async-start(), calls=%async_computation.19 | async-start | bytes 1179648 | tf_op jit(solution)/shard_map/psum | solution.py:264
  1070.5 357.6 %all-reduce.14.cloned.1.call-start = ((), (), s32[]{:S(2)}) async-start(), calls=%async_computation.26 | async-start | bytes 12976128 | tf_op jit(solution)/shard_map/psum | solution.py:265
  1140.3 1.9 copy-start.39
  1140.3 3.2 copy-start.34
  1168.5 5.0 copy-start.23
  1172.6 2.7 copy-start.14
  1172.6 2.7 copy-start.24
  1428.0 2.3 copy-start.30
  1428.0 3.3 copy-start.29
  1430.3 2.2 copy-start.19
  1432.5 2.8 copy-start.18
  (13 other events, 14.6 us)
Sparse Core Ops, SparseCore 0:
  9.6 11.9 all-gather.8
  23.1 10.3 all-gather.10
  35.0 10.3 all-gather.12
  46.9 10.3 all-gather.14
  58.7 15.5 all-gather.16
  75.7 15.6 all-gather.18
  968.6 8.0 reduce-scatter.15
  979.6 24.4 reduce-scatter.11
  1007.1 22.5 reduce-scatter.13
  1032.0 38.3 all-reduce.9
  1073.4 8.3 reduce-scatter.21
  1084.4 9.8 reduce-scatter.17
  1097.2 9.8 reduce-scatter.19
  1109.8 13.7 reduce-scatter.23
  1126.5 13.7 reduce-scatter.25
  1142.9 8.5 reduce-scatter.27
  1154.3 47.4 all-reduce.11
  1209.2 218.7 all-reduce.13
